TPU v7x, 32 devices: a whole 2x2x4 slice. The times are simulated.
32 devices in a mesh: dp: 4 (over y, x), shard: 4 (over z), rep: 2 (over core).
Axes of the slice: x: 2, y: 2, z: 4, core: 2. Of those that a mesh axis runs over, the one named last changes fastest.
Arguments:
- earlier_precise_parameters: float32 [8, 512, 128], P(('dp', 'rep'), 'shard'), may hold values from -6 to 6
- earlier_mean_estimate: float32 [8, 512, 128], P(('dp', 'rep'), 'shard'), may hold values from -6 to 6
- earlier_variance_estimate: float32 [8, 512, 128], P(('dp', 'rep'), 'shard'), may hold values from 0.01 to 10
- replica_slope_portions: bfloat16 [8, 8192, 128], P(('dp', 'rep'), 'shard'), may hold values from -6 to 6
- segment_fresh_owner: int32 [4, 4], replicated, may hold values from 0 to 3, as said below
- segment_line_lengths: int32 [4, 4], replicated, may hold values from 0 to 64, as said below
- remaining_worker: int32 [4], replicated, may hold values from 0 to 3, each once
Outputs:
- master_new: float32 [8, 1024, 128], P(('dp', 'rep'), 'shard')
- moment_new: float32 [8, 1024, 128], P(('dp', 'rep'), 'shard')
- second_new: float32 [8, 1024, 128], P(('dp', 'rep'), 'shard')
Inputs may be any that keep to these rules, and one draw needn't show every extreme that they name: `segment_fresh_owner`: each row lists every new owner once. `segment_line_lengths`: each row sums to 128; one new owner, drawn anew, receives exactly 64 rows from every old rank, 256 in all; the blocks of any other owner hold at most 256 rows over all old ranks. `remaining_worker`: each old rank once.
All inputs are finite; a program needn't handle non-finite values.
Results may differ from a plain program's by a relative error of at most 0.0003.
Values sent between devices are 32-bit elements; how exact they have to be, the bound alone decides.
No kernel may reach another device: no remote copies, remote signals or barrier semaphores. Data moves between devices by JAX's collectives and lax.ppermute only.
A program may use at most 64 MiB of HBM per device.

v0:
```python
import jax
import jax.numpy as jnp
from jax import lax
from jax.sharding import PartitionSpec as P

beta_first = 0.9
beta_second = 0.95
bias_first = 1.0 - 0.9**50
bias_second = 1.0 - 0.95**50
epsilon_adam = 1e-08
decay_rate = 0.1
learn_rate = 0.0003


def block_tables(segment_fresh_owner, segment_line_lengths, shard_count):
    block_starts = jnp.cumsum(segment_line_lengths, axis=1) - segment_line_lengths
    peers = jnp.arange(shard_count, dtype=jnp.int32)
    pair_rows = jnp.sum(
        jnp.where(
            segment_fresh_owner[:, :, None] == peers[None, None, :],
            segment_line_lengths[:, :, None],
            0,
        ),
        axis=1,
    )
    pair_offset = jnp.cumsum(pair_rows, axis=0) - pair_rows
    return (block_starts, pair_rows, pair_offset)


def locate_rows(ranks, inner, segment_fresh_owner, segment_line_lengths, block_starts):
    rank_starts = block_starts[ranks]
    rank_ends = rank_starts + segment_line_lengths[ranks]
    block_index = jnp.sum((rank_ends <= inner[:, None]).astype(jnp.int32), axis=1)
    owner = jnp.take_along_axis(segment_fresh_owner[ranks], block_index[:, None], axis=1)[:, 0]
    offset = inner - jnp.take_along_axis(rank_starts, block_index[:, None], axis=1)[:, 0]
    return (owner, offset)


def adam_update(weights, first, squares, gradient, live):
    moment = beta_first * first + (1.0 - beta_first) * gradient
    second = beta_second * squares + (1.0 - beta_second) * gradient * gradient
    update = (
        moment / bias_first / (jnp.sqrt(second / bias_second) + epsilon_adam) + decay_rate * weights
    )
    new_weights = weights - learn_rate * update
    keep = live.astype(jnp.float32)[:, None]
    return (new_weights * keep, moment * keep, second * keep)


def local(
    earlier_precise_parameters,
    earlier_mean_estimate,
    earlier_variance_estimate,
    replica_slope_portions,
    segment_fresh_owner,
    segment_line_lengths,
    remaining_worker,
):
    shard_count = lax.axis_size("shard")
    own_position = lax.axis_index("shard")
    old_count = earlier_precise_parameters.shape[1]
    width = earlier_precise_parameters.shape[2]
    capacity = 2 * old_count
    slot_rows = capacity // shard_count
    stacked = jnp.concatenate(
        [earlier_precise_parameters[0], earlier_mean_estimate[0], earlier_variance_estimate[0]],
        axis=1,
    )
    block_starts, pair_rows, pair_offset = block_tables(
        segment_fresh_owner, segment_line_lengths, shard_count
    )
    vertical_line_tally = jnp.take(pair_rows, own_position, axis=1)
    vertical_displacement = jnp.take(pair_offset, own_position, axis=1)
    empty = jnp.zeros((capacity, 3 * width), jnp.float32)
    present_worker = remaining_worker[own_position]
    local_rows = jnp.arange(old_count, dtype=jnp.int32)
    owner, offset = locate_rows(
        jnp.zeros((old_count,), jnp.int32) + present_worker,
        local_rows,
        segment_fresh_owner,
        segment_line_lengths,
        block_starts,
    )
    outgoing = (
        jnp.zeros((shard_count * slot_rows, 3 * width), jnp.float32)
        .at[owner * slot_rows + offset]
        .set(stacked)
    )
    incoming = lax.all_to_all(outgoing, "shard", split_axis=0, concat_axis=0, tiled=True)
    received_lines = vertical_line_tally[remaining_worker]
    landing_position = vertical_displacement[remaining_worker]
    slot_pos = jnp.arange(slot_rows, dtype=jnp.int32)
    target = jnp.where(
        slot_pos[None, :] < received_lines[:, None],
        landing_position[:, None] + slot_pos[None, :],
        capacity,
    ).reshape(-1)
    placed = empty.at[target].set(incoming, mode="drop")
    grad_terms = replica_slope_portions.astype(jnp.float32)
    gradient = lax.psum_scatter(grad_terms, ("dp", "rep"), scatter_dimension=1, tiled=True)
    total_here = jnp.sum(vertical_line_tally)
    live = jnp.arange(capacity, dtype=jnp.int32) < total_here
    weights = placed[:, :width]
    first = placed[:, width : 2 * width]
    squares = placed[:, 2 * width :]
    new_weights, moment, second = adam_update(weights, first, squares, gradient[0], live)
    return (new_weights[None], moment[None], second[None])


def solution(mesh):
    in_specs = (
        P(("dp", "rep"), "shard", None),
        P(("dp", "rep"), "shard", None),
        P(("dp", "rep"), "shard", None),
        P(("dp", "rep"), "shard", None),
        P(),
        P(),
        P(),
    )
    out_specs = (
        P(("dp", "rep"), "shard", None),
        P(("dp", "rep"), "shard", None),
        P(("dp", "rep"), "shard", None),
    )
    return jax.shard_map(local, mesh=mesh, in_specs=in_specs, out_specs=out_specs, check_vma=False)
```

profile of v0, /device:TPU:0, one launch (start us, length us, event | category | flops | bytes accessed | tf_op | source)
XLA Modules:
  0.0 58.5 jit_solution(6648181498857198718)
XLA Ops:
  7.2 2.1 %convert_element_type.14 = f32[1,2048,128]{2,1,0:T(8,128)} convert(bf16[1,2048,128]{2,1,0:T(8,128)(2,1)} %param.14) | non-fusion elementwise | flops 262144 | bytes 1572864 | tf_op jit(solution)/shard_map/convert_element_type | solution.py:99
  9.4 0.6 %copy-done.5 = s32[4]{0:T(128)S(1)} copy-done((s32[4]{0:T(128)S(1)}, s32[4]{0:T(128)}, u32[]{:S(2)}) %copy-start.5) | copy-done | bytes 40
  10.0 0.6 dynamic_slice.3
  11.9 0.2 reduce_window_sum.23
  12.8 0.6 %gather_fusion.4 = s32[128,4]{1,0:T(8,128)S(1)} fusion(s32[4,4]{1,0:T(4,128)S(1)} %copy-done, s32[1024]{0:T(1024)S(1)} %pad_clamp_fusion), kind=kCustom, calls=%fused_computation.6 | custom fusion | bytes 4608 | tf_op jit(solution)/shard_map/gather | solution.py:32
  13.4 0.6 %gather_fusion.3 = s32[128,4]{1,0:T(8,128)S(1)} fusion(s32[4,4]{1,0:T(4,128)S(1)} %sub.14, s32[1024]{0:T(1024)S(1)} %pad_clamp_fusion), kind=kCustom, calls=%fused_computation.5 | custom fusion | bytes 4608 | tf_op jit(solution)/shard_map/gather | solution.py:31
  14.1 0.1 convert_reduce_fusion
  14.2 1.3 %gather_fusion.6 = s32[128]{0:T(128)S(1)} fusion(s32[128,4]{1,0:T(8,128)S(1)} %gather_fusion.3, s32[128]{0:T(128)S(1)} %or_bitcast_fusion), kind=kCustom, calls=%fused_computation.1.clone | custom fusion | bytes 2048 | tf_op jit(solution)/shard_map/jit(take_along_axis)/gather | solution.py:35
  15.5 0.6 %gather_fusion.2 = s32[128,4]{1,0:T(8,128)S(1)} fusion(s32[4,4]{1,0:T(4,128)S(1)} %copy-done.1, s32[1024]{0:T(1024)S(1)} %pad_clamp_fusion), kind=kCustom, calls=%fused_computation.4 | custom fusion | bytes 4608 | tf_op jit(solution)/shard_map/gather | solution.py:34
  16.2 1.3 %gather_fusion.5 = s32[128]{0:T(128)S(1)} fusion(s32[128,4]{1,0:T(8,128)S(1)} %gather_fusion.2, s32[128]{0:T(128)S(1)} %or_bitcast_fusion), kind=kCustom, calls=%fused_computation.clone | custom fusion | bytes 2048 | tf_op jit(solution)/shard_map/jit(take_along_axis)/gather | solution.py:34
  17.5 1.7 %scatter_custom_fusion = f32[256,384]{1,0:T(8,128)} fusion(s32[128]{0:T(128)S(1)} %fusion.11, f32[128,128]{1,0:T(8,128)S(1)} %bitcast.57, f32[]{:T(128)} %constant.137, f32[128,128]{1,0:T(8,128)S(1)} %bitcast.58, f32[128,128]{1,0:T(8,128)S(1)} %bitcast.59, f32[]{:T(128)} %constant.14.clone.1), kind=kCustom, calls=%fused_computation.9 | custom fusion | flops 98304 | bytes 589832 | tf_op jit(solution)/shard_map/scatter | solution.py:87
  19.3 6.3 %all-to-all-start = ((f32[4,64,384]{2,1,0:T(8,128)}), f32[4,64,384]{2,1,0:T(8,128)S(1)}, u32[]{:S(2)}, u32[]{:S(2)}) async-start(f32[4,64,384]{2,1,0:T(8,128)} %bitcast.12), calls=%async_computation | async-start | bytes 786432 | tf_op jit(solution)/shard_map/all_to_all | solution.py:89
  25.6 0.1 select_reduce_fusion
  25.8 0.2 select_reduce_fusion.1
  26.0 0.6 %reduce_sum.29 = s32[]{:T(128)} reduce(s32[4]{0:T(128)S(1)} %get-tuple-element.20, s32[]{:T(128)} %constant.15.clone.1), dimensions={0}, to_apply=%region_7.10 | reduce | flops 3 | bytes 24 | tf_op jit(solution)/shard_map/reduce_sum | solution.py:101
  26.6 0.6 %gather_fusion = s32[4]{0:T(128)S(1)} fusion(s32[4]{0:T(128)S(1)} %get-tuple-element.20, s32[1024]{0:T(1024)S(1)} %pad_clamp_fusion.1), kind=kCustom, calls=%fused_computation.2 | custom fusion | bytes 48 | tf_op jit(solution)/shard_map/gather | solution.py:90
  27.3 0.6 %gather_fusion.1 = s32[4]{0:T(128)S(1)} fusion(s32[4]{0:T(128)S(1)} %get-tuple-element.19, s32[1024]{0:T(1024)S(1)} %pad_clamp_fusion.1), kind=kCustom, calls=%fused_computation.3 | custom fusion | bytes 48 | tf_op jit(solution)/shard_map/gather | solution.py:91
  27.9 0.1 add_select_fusion
  28.0 0.1 select_n.64
  28.1 0.7 %compare_convert_fusion = f32[256]{0:T(256)S(1)} fusion(s32[]{:T(128)} %reduce_sum.29), kind=kLoop, calls=%fused_computation.42 | loop fusion | flops 512 | bytes 1028 | tf_op jit(solution)/shard_map/convert_element_type | solution.py:46
  28.7 8.6 %all-to-all-done = f32[4,64,384]{2,1,0:T(8,128)S(1)} async-done(((f32[4,64,384]{2,1,0:T(8,128)}), f32[4,64,384]{2,1,0:T(8,128)S(1)}, u32[]{:S(2)}, u32[]{:S(2)}) %all-to-all-start) | async-done | bytes 393248 | tf_op jit(solution)/shard_map/all_to_all | solution.py:89
  37.3 1.5 %scatter_custom_fusion.1 = f32[256,384]{1,0:T(8,128)S(1)} fusion(s32[256]{0:T(256)S(1)} %bitcast.60, f32[256,384]{1,0:T(8,128)S(1)} %bitcast.56, f32[]{:T(128)} %constant.14.clone.1), kind=kCustom, calls=%fused_computation.16 | custom fusion | bytes 393220 | tf_op jit(solution)/shard_map/scatter | solution.py:98
  38.8 11.0 %reduce-scatter.2.cloned.1.call-done = f32[1,256,128]{2,1,0:T(8,128)} async-done(((f32[1,2048,128]{2,1,0:T(8,128)}), f32[1,256,128]{2,1,0:T(8,128)}) %reduce-scatter.2.cloned.1.call-update) | async-done | bytes 131088 | tf_op jit(solution)/shard_map/reduce_scatter | solution.py:100
  49.9 1.8 %multiply_bitcast_fusion = (f32[1,256,128]{2,1,0:T(8,128)}, f32[1,256,128]{2,1,0:T(8,128)}, f32[1,256,128]{2,1,0:T(8,128)}) fusion(f32[256]{0:T(256)S(1)} %compare_convert_fusion, f32[1,256,128]{2,1,0:T(8,128)} %reduce-scatter.2.cloned.1.call-done, f32[256,384]{1,0:T(8,128)S(1)} %scatter_custom_fusion.1), kind=kLoop, calls=%fused_computation.24 | loop fusion | flops 589824 | bytes 918528 | tf_op jit(solution)/shard_map/broadcast_in_dim | solution.py:107
  (26 shorter events, 0.2 us)
Async XLA Ops:
  7.2 42.7 %reduce-scatter.2.cloned.1.call-start = ((), (), s32[]{:S(2)}) async-start(), calls=%async_computation.2 | async-start | bytes 1179648 | tf_op jit(solution)/shard_map/reduce_scatter | solution.py:100
  9.3 0.7 %copy-start.5 = (s32[4]{0:T(128)S(1)}, s32[4]{0:T(128)}, u32[]{:S(2)}) copy-start(s32[4]{0:T(128)} %param.17) | copy-start | bytes 52
  10.6 1.3 %copy-start = (s32[4,4]{1,0:T(4,128)S(1)}, s32[4,4]{1,0:T(4,128)}, u32[]{:S(2)}) copy-start(s32[4,4]{1,0:T(4,128)} %param.16) | copy-start | bytes 196
  14.2 1.3 %copy-start.1 = (s32[4,4]{1,0:T(4,128)S(1)}, s32[4,4]{1,0:T(4,128)}, u32[]{:S(2)}) copy-start(s32[4,4]{1,0:T(4,128)} %param.15) | copy-start | bytes 196
  16.2 1.3 %copy-start.2 = (f32[1,128,128]{2,1,0:T(8,128)S(1)}, f32[1,128,128]{2,1,0:T(8,128)}, u32[]{:S(2)}) copy-start(f32[1,128,128]{2,1,0:T(8,128)} %param.13) | copy-start | bytes 196612
  16.2 1.3 %copy-start.3 = (f32[1,128,128]{2,1,0:T(8,128)S(1)}, f32[1,128,128]{2,1,0:T(8,128)}, u32[]{:S(2)}) copy-start(f32[1,128,128]{2,1,0:T(8,128)} %param.12) | copy-start | bytes 196612
  16.2 1.3 %copy-start.4 = (f32[1,128,128]{2,1,0:T(8,128)S(1)}, f32[1,128,128]{2,1,0:T(8,128)}, u32[]{:S(2)}) copy-start(f32[1,128,128]{2,1,0:T(8,128)} %param.11) | copy-start | bytes 196612
  19.3 18.0 %all-to-all-start = ((f32[4,64,384]{2,1,0:T(8,128)}), f32[4,64,384]{2,1,0:T(8,128)S(1)}, u32[]{:S(2)}, u32[]{:S(2)}) async-start(f32[4,64,384]{2,1,0:T(8,128)} %bitcast.12), calls=%async_computation | async-start | bytes 786432 | tf_op jit(solution)/shard_map/all_to_all | solution.py:89
Sparse Core Ops, SparseCore 0:
  11.1 38.6 reduce-scatter.1
where the time goes:
time: 58.8 us; the launch traced here: 58.5 us
  waiting for transfers between devices  19.6 us (33%)
  between operations  16.2 us (28%)
  local copies, waits for them, and re-layouts  8.62 us (15%)
  other arithmetic  7.67 us (13%)
  starting transfers between devices  6.38 us (11%)
    reduce_scatter x1, waiting for transfers between devices, local(): lax.psum_scatter(grad_terms, ('dp', 'rep'), scatter_dimension=1, tiled=True)  11 us
    all_to_all x1, waiting for transfers between devices, local(): lax.all_to_all(outgoing, 'shard', split_axis=0, concat_axis=0, tiled=True)  8.56 us
    all_to_all x1, starting transfers between devices, local(): lax.all_to_all(outgoing, 'shard', split_axis=0, concat_axis=0, tiled=True)  6.35 us
    convert_element_type x1, other arithmetic, local(): grad_terms = replica_slope_portions.astype(jnp.float32)  2.1 us
    broadcast_in_dim x1, other arithmetic, local(): return (new_weights[None], moment[None], second[None])  1.76 us
    scatter x1, other arithmetic, local(): outgoing = jnp.zeros((shard_count * slot_rows, 3 * width), jnp.float32).a...  1.75 us
    scatter x1, local copies, waits for them, and re-layouts, local(): placed = empty.at[target].set(incoming, mode='drop')  1.52 us
    gather x1, local copies, waits for them, and re-layouts, locate_rows(): jnp.take_along_axis(segment_fresh_owner[ranks], block_index[:, None], axi...  1.27 us
  transfers between devices with their start and end apart: 2, of which 2 were waited for; matrix products, arithmetic and copies ran while one was open for 20% of the time, Pallas kernels for 0%

commit v1 on v0

v1 whole, which is shorter than its diff:
```python
import functools

import jax
import jax.numpy as jnp
from jax import lax
from jax.experimental import pallas as pl
from jax.experimental.pallas import tpu as pltpu
from jax.sharding import PartitionSpec as P

beta_first = 0.9
beta_second = 0.95
bias_first = 1.0 - 0.9**50
bias_second = 1.0 - 0.95**50
epsilon_adam = 1e-08
decay_rate = 0.1
learn_rate = 0.0003

DIRECT_PEERS = 8
PARAMS = pltpu.CompilerParams(vmem_limit_bytes=16 * 2**20)

VMEM = pl.BlockSpec(memory_space=pltpu.VMEM)
SMEM = pl.BlockSpec(memory_space=pltpu.SMEM)


def peer(index, turn, count):
    return index ^ turn if count & (count - 1) == 0 else lax.rem(index + turn, count)


def origin(index, turn, count):
    return index ^ turn if count & (count - 1) == 0 else lax.rem(index + count - turn, count)


def route(turn, count):
    if count & (count - 1) == 0:
        return [(i, i ^ turn) for i in range(count)]
    return [(i, (i + turn) % count) for i in range(count)]


def exchange(value, axis, turn):
    return lax.ppermute(value, axis, route(turn, lax.axis_size(axis)))


def loop(count, body):
    if count <= DIRECT_PEERS:
        for step in range(count):
            body(step)
    else:
        lax.fori_loop(0, count, lambda step, _: (body(step), 0)[1], 0)


def pack_kernel(count, slot, owner, lengths, worker, w, m, v, *rest):
    outs, (padded, starts) = rest[:-2], rest[-2:]
    rows = w.shape[1]
    me = lax.axis_index("shard")
    rank = worker[me]

    def place(block, start):
        starts[owner[rank, block]] = start
        return start + lengths[rank, block]

    start = jnp.int32(0)
    if count <= DIRECT_PEERS:
        for block in range(count):
            start = place(block, start)
    else:
        lax.fori_loop(0, count, place, start)
    for part, ref in enumerate((w, m, v)):
        padded[part, pl.ds(0, rows), :] = ref[0]
        padded[part, pl.ds(rows, padded.shape[1] - rows), :] = jnp.zeros(
            (padded.shape[1] - rows, ref.shape[2]), jnp.float32
        )
    if len(outs) == count:
        for turn in range(count):
            first = starts[peer(me, turn, count)]
            for part in range(3):
                outs[turn][part] = padded[part, pl.ds(first, slot), :]
    else:

        def fill(dest):
            first = starts[dest]
            for part in range(3):
                outs[0][dest, part] = padded[part, pl.ds(first, slot), :]

        loop(count, fill)


def pack(count, slot, owner, lengths, worker, w, m, v):
    rows, width = w.shape[1:]
    direct = count <= DIRECT_PEERS
    shape = (3, slot, width)
    out = [jax.ShapeDtypeStruct(shape, jnp.float32)] * count if direct else [jax.ShapeDtypeStruct((count,) + shape, jnp.float32)]
    return pl.pallas_call(
        functools.partial(pack_kernel, count, slot),
        out_shape=out,
        in_specs=[SMEM] * 3 + [VMEM] * 3,
        out_specs=[VMEM] * len(out),
        scratch_shapes=[
            pltpu.VMEM((3, rows + max(slot, 8), width), jnp.float32),
            pltpu.SMEM((count,), jnp.int32),
        ],
        compiler_params=PARAMS,
        name="pack",
    )(owner, lengths, worker, w, m, v)


def widen_kernel(reps, grads, *outs):
    me = lax.axis_index("rep")
    for turn in range(1, reps):
        theirs = peer(me, turn, reps)
        for block in range(grads.shape[0]):
            outs[turn - 1][block] = grads[block, theirs].astype(jnp.float32)


def widen(reps, grads):
    blocks, _, rows, width = grads.shape
    return pl.pallas_call(
        functools.partial(widen_kernel, reps),
        out_shape=[jax.ShapeDtypeStruct((blocks, rows, width), jnp.float32)] * (reps - 1),
        in_specs=[VMEM],
        out_specs=[VMEM] * (reps - 1),
        compiler_params=PARAMS,
        name="widen",
    )(grads)


def fold_kernel(reps, count, grads, *refs):
    arrived, outs = refs[: reps - 1], refs[reps - 1 :]
    rep = lax.axis_index("rep")
    me = lax.axis_index("dp")
    for turn in range(count):
        block = peer(me, turn, count)
        total = grads[block, rep].astype(jnp.float32)
        for ref in arrived:
            total += ref[block]
        outs[turn][...] = total


def fold(reps, grads, arrived):
    count, _, rows, width = grads.shape
    return pl.pallas_call(
        functools.partial(fold_kernel, reps, count),
        out_shape=[jax.ShapeDtypeStruct((rows, width), jnp.float32)] * count,
        in_specs=[VMEM] * reps,
        out_specs=[VMEM] * count,
        compiler_params=PARAMS,
        name="fold",
    )(grads, *arrived)


def adam_kernel(count, parts, slot, owner, lengths, worker, *refs):
    n_chunks = count if count <= DIRECT_PEERS else 1
    chunks = refs[:n_chunks]
    sums = refs[n_chunks : n_chunks + parts]
    new_w, new_m, new_v, placed, where = refs[n_chunks + parts :]
    capacity = new_w.shape[1]
    me = lax.axis_index("shard")

    def locate(position):
        where[worker[position]] = position

    loop(count, locate)

    def rows_of(rank):
        if count <= DIRECT_PEERS:
            total = jnp.int32(0)
            for block in range(count):
                total += jnp.where(owner[rank, block] == me, lengths[rank, block], 0)
            return total
        return lax.fori_loop(
            0, count, lambda b, t: t + jnp.where(owner[rank, b] == me, lengths[rank, b], 0), jnp.int32(0)
        )

    if count <= DIRECT_PEERS:
        total = jnp.int32(0)
        for rank in range(count):
            source = where[rank]
            for turn in range(count):

                @pl.when(origin(me, turn, count) == source)
                def _():
                    for part in range(3):
                        placed[part, pl.ds(total, slot), :] = chunks[turn][part]

            total += rows_of(rank)
    else:

        def put(rank, total):
            for part in range(3):
                placed[part, pl.ds(total, slot), :] = chunks[0][where[rank], part]
            return total + rows_of(rank)

        total = lax.fori_loop(0, count, put, jnp.int32(0))

    gradient = sums[0][...]
    for ref in sums[1:]:
        gradient += ref[...]
    live = lax.broadcasted_iota(jnp.int32, gradient.shape, 0) < total
    weights = placed[0, :capacity, :]
    moment = beta_first * placed[1, :capacity, :] + (1.0 - beta_first) * gradient
    second = beta_second * placed[2, :capacity, :] + (1.0 - beta_second) * gradient * gradient
    update = (
        moment / bias_first / (jnp.sqrt(second / bias_second) + epsilon_adam) + decay_rate * weights
    )
    new_w[0] = jnp.where(live, weights - learn_rate * update, 0.0)
    new_m[0] = jnp.where(live, moment, 0.0)
    new_v[0] = jnp.where(live, second, 0.0)


def adam(count, slot, owner, lengths, worker, chunks, sums):
    capacity, width = sums[0].shape
    out = jax.ShapeDtypeStruct((1, capacity, width), jnp.float32)
    return pl.pallas_call(
        functools.partial(adam_kernel, count, len(sums), slot),
        out_shape=[out] * 3,
        in_specs=[SMEM] * 3 + [VMEM] * (len(chunks) + len(sums)),
        out_specs=[VMEM] * 3,
        scratch_shapes=[
            pltpu.VMEM((3, capacity + max(slot, 8), width), jnp.float32),
            pltpu.SMEM((count,), jnp.int32),
        ],
        compiler_params=PARAMS,
        name="adam",
    )(owner, lengths, worker, *chunks, *sums)


def local(w, m, v, portions, owner, lengths, worker):
    shards = lax.axis_size("shard")
    groups = lax.axis_size("dp")
    reps = lax.axis_size("rep")
    capacity = portions.shape[1] // (groups * reps)
    slot = capacity // shards
    grads = portions.reshape(groups, reps, capacity, portions.shape[2])

    halves = widen(reps, grads)
    arrived = [exchange(halves[t - 1], "rep", t) for t in range(1, reps)]
    packed = pack(shards, slot, owner, lengths, worker, w, m, v)
    if shards <= DIRECT_PEERS:
        chunks = [packed[0]] + [exchange(packed[t], "shard", t) for t in range(1, shards)]
    else:
        chunks = [lax.all_to_all(packed[0], "shard", 0, 0, tiled=True)]
    folded = fold(reps, grads, arrived)
    sums = [folded[0]] + [exchange(folded[t], "dp", t) for t in range(1, groups)]
    return tuple(adam(shards, slot, owner, lengths, worker, chunks, sums))


def solution(mesh):
    split = P(("dp", "rep"), "shard", None)
    return jax.shard_map(
        local,
        mesh=mesh,
        in_specs=(split,) * 4 + (P(),) * 3,
        out_specs=(split,) * 3,
        check_vma=False,
    )
```

time: 58.8 us -> 21.4 us (0.36)
  between operations: 16.2 us -> 0.71 us
  waiting for transfers between devices: 19.6 us -> 6.56 us
  other arithmetic: 7.67 us -> 0 us
  local copies, waits for them, and re-layouts: 8.62 us -> 1.31 us
  starting transfers between devices: 6.38 us -> 10.3 us
  Pallas kernels: 0 us -> 2.34 us
    reduce_scatter x1 -> x0, waiting for transfers between devices: 11 us -> none  [local(): lax.psum_scatter(grad_terms, ('dp', 'rep'), scatter_dimension=1, tiled=True)]
    ppermute x0 -> x7, starting transfers between devices: none -> 10.3 us  [exchange(): return lax.ppermute(value, axis, route(turn, lax.axis_size(axis)))]
    all_to_all x1 -> x0, waiting for transfers between devices: 8.56 us -> none  [local(): lax.all_to_all(outgoing, 'shard', split_axis=0, concat_axis=0, tiled=True)]
    ppermute x0 -> x7, waiting for transfers between devices: none -> 6.56 us  [exchange(): return lax.ppermute(value, axis, route(turn, lax.axis_size(axis)))]
    all_to_all x1 -> x0, starting transfers between devices: 6.35 us -> none  [local(): lax.all_to_all(outgoing, 'shard', split_axis=0, concat_axis=0, tiled=True)]
    gather x7 -> x0, local copies, waits for them, and re-layouts: 5.75 us -> none  [the longest x1 1.27 us: locate_rows(): jnp.take_along_axis(segment_fresh_owner[ranks], block_index[:, None], axi...]
    convert_element_type x2 -> x0, other arithmetic: 2.75 us -> none  [the longest x1 2.1 us: local(): grad_terms = replica_slope_portions.astype(jnp.float32)]
    pallas_call x0 -> x4, Pallas kernels: none -> 2.34 us  [the longest x1 1.6 us: adam(): pl.pallas_call(functools.partial(adam_kernel, count, len(sums), slot), ou...]
  transfers between devices with their start and end apart: 2 -> 7, of which waited for: 2 -> 1; matrix products, arithmetic and copies ran while one was open for 20% -> 0% of each run, Pallas kernels for 0% -> 3%
where the time goes in v1:
time: 21.4 us; the launch traced here: 21.2 us
  starting transfers between devices  10.3 us (48%)
  waiting for transfers between devices  6.56 us (31%)
  Pallas kernels  2.34 us (11%)
  local copies, waits for them, and re-layouts  1.31 us (6%)
  between operations  0.71 us (3%)
    ppermute x7, starting transfers between devices, exchange(): return lax.ppermute(value, axis, route(turn, lax.axis_size(axis)))  10.3 us
    ppermute x7, waiting for transfers between devices, exchange(): return lax.ppermute(value, axis, route(turn, lax.axis_size(axis)))  6.56 us
    pallas_call x1, Pallas kernels, adam(): pl.pallas_call(functools.partial(adam_kernel, count, len(sums), slot), ou...  1.6 us
    unnamed x16, local copies, waits for them, and re-layouts  1.31 us
    pallas_call x1, Pallas kernels, pack(): pl.pallas_call(functools.partial(pack_kernel, count, slot), out_shape=out...  0.65 us
  transfers between devices with their start and end apart: 7, of which 1 were waited for; matrix products, arithmetic and copies ran while one was open for 0% of the time, Pallas kernels for 3%

profile of v1, /device:TPU:0, one launch (start us, length us, event | category | flops | bytes accessed | tf_op | source)
XLA Modules:
  0.0 21.2 jit_solution(17899824953758232760)
XLA Ops:
  0.6 0.0 copy-start
  0.6 1.0 %copy-done = bf16[1,2048,128]{2,1,0:T(8,128)(2,1)S(1)} copy-done((bf16[1,2048,128]{2,1,0:T(8,128)(2,1)S(1)}, bf16[1,2048,128]{2,1,0:T(8,128)(2,1)}, u32[]{:S(2)}) %copy-start) | copy-done | bytes 524312
  1.7 0.0 copy-start.6
  1.7 0.0 copy-start.7
  1.7 0.0 copy-start.1
  1.8 0.6 %collective-permute-start.3 = (f32[4,256,128]{2,1,0:T(8,128)S(1)}, f32[4,256,128]{2,1,0:T(8,128)S(1)}, u32[]{:S(2)}, u32[]{:S(2)}) collective-permute-start(f32[4,256,128]{2,1,0:T(8,128)S(1)} %widen.1), channel_id=1, source_target_pairs={{0,1},{1,0},{2,3},{3,2},{4,5},{5,4},{6,7},{7,6},{8,9},{9,8},{10,11... | collective-permute-start | bytes 1572872 | tf_op jit(solution)/shard_map/ppermute | solution.py:40
  2.3 0.2 copy-done.2
  2.5 0.0 copy-done.3
  2.5 0.0 copy-done.4
  2.6 0.7 %pack.1 = (f32[3,64,128]{2,1,0:T(8,128)S(1)}, f32[3,64,128]{2,1,0:T(8,128)S(1)}, f32[3,64,128]{2,1,0:T(8,128)S(1)}, f32[3,64,128]{2,1,0:T(8,128)S(1)}) custom-call(s32[4,4]{1,0:T(4,128)S(1)} %copy-done.5, s32[4,4]{1,0:T(4,128)S(1)} %copy-done.6, s32[4]{0:T(128)S(1)} %copy-done.7, f32[1,128,128]{2,1,0:T(8,128)S(1)} %copy-done.2, ...), custom_call_target="tpu_custom_call" | custom-call | tf_op jit(solution)/shard_map/pack/pallas_call | solution.py:92
  3.2 3.1 %collective-permute-start = (f32[3,64,128]{2,1,0:T(8,128)S(1)}, f32[3,64,128]{2,1,0:T(8,128)S(1)}, u32[]{:S(2)}, u32[]{:S(2)}) collective-permute-start(f32[3,64,128]{2,1,0:T(8,128)S(1)} %get-tuple-element.12), channel_id=1, source_target_pairs={{0,2},{2,0},{4,6},{6,4},{1,3},{3,1},{5,7},{7,5},{8,10},{10,8},{12,... | collective-permute-start | bytes 294920 | tf_op jit(solution)/shard_map/ppermute | solution.py:40
  6.4 0.0 collective-permute-done.3.refs_0_
  6.4 1.6 %collective-permute-start.4 = (f32[256,128]{1,0:T(8,128)S(1)}, f32[256,128]{1,0:T(8,128)S(1)}, u32[]{:S(2)}, u32[]{:S(2)}) collective-permute-start(f32[256,128]{1,0:T(8,128)S(1)} %get-tuple-element.16), channel_id=1, source_target_pairs={{0,8},{8,0},{16,24},{24,16},{1,9},{9,1},{17,25},{25,17},{2,10},{10... | collective-permute-start | bytes 393224 | tf_op jit(solution)/shard_map/ppermute | solution.py:40
  8.0 1.5 %collective-permute-start.5 = (f32[256,128]{1,0:T(8,128)S(1)}, f32[256,128]{1,0:T(8,128)S(1)}, u32[]{:S(2)}, u32[]{:S(2)}) collective-permute-start(f32[256,128]{1,0:T(8,128)S(1)} %get-tuple-element.17), channel_id=1, source_target_pairs={{0,16},{8,24},{16,0},{24,8},{1,17},{9,25},{17,1},{25,9},{2,18},{10... | collective-permute-start | bytes 393224 | tf_op jit(solution)/shard_map/ppermute | solution.py:40
  9.5 0.5 %collective-permute-start.6 = (f32[256,128]{1,0:T(8,128)S(1)}, f32[256,128]{1,0:T(8,128)S(1)}, u32[]{:S(2)}, u32[]{:S(2)}) collective-permute-start(f32[256,128]{1,0:T(8,128)S(1)} %get-tuple-element.18), channel_id=1, source_target_pairs={{0,24},{8,16},{16,8},{24,0},{1,25},{9,17},{17,9},{25,1},{2,26},{10... | collective-permute-start | bytes 393224 | tf_op jit(solution)/shard_map/ppermute | solution.py:40
  10.0 2.6 %collective-permute-start.1 = (f32[3,64,128]{2,1,0:T(8,128)S(1)}, f32[3,64,128]{2,1,0:T(8,128)S(1)}, u32[]{:S(2)}, u32[]{:S(2)}) collective-permute-start(f32[3,64,128]{2,1,0:T(8,128)S(1)} %get-tuple-element.13), channel_id=1, source_target_pairs={{0,4},{2,6},{4,0},{6,2},{1,5},{3,7},{5,1},{7,3},{8,12},{10,14},{12... | collective-permute-start | bytes 294920 | tf_op jit(solution)/shard_map/ppermute | solution.py:40
  12.6 0.0 collective-permute-done.refs_1_
  12.6 0.4 %collective-permute-start.2 = (f32[3,64,128]{2,1,0:T(8,128)S(1)}, f32[3,64,128]{2,1,0:T(8,128)S(1)}, u32[]{:S(2)}, u32[]{:S(2)}) collective-permute-start(f32[3,64,128]{2,1,0:T(8,128)S(1)} %get-tuple-element.14), channel_id=1, source_target_pairs={{0,6},{2,4},{4,2},{6,0},{1,7},{3,5},{5,3},{7,1},{8,14},{10,12},{12... | collective-permute-start | bytes 294920 | tf_op jit(solution)/shard_map/ppermute | solution.py:40
  13.0 6.5 %collective-permute-done.1.refs_2_ = f32[3,64,128]{2,1,0:T(8,128)S(1)} collective-permute-done((f32[3,64,128]{2,1,0:T(8,128)S(1)}, f32[3,64,128]{2,1,0:T(8,128)S(1)}, u32[]{:S(2)}, u32[]{:S(2)}) %collective-permute-start.1) | collective-permute-done | bytes 98336 | tf_op jit(solution)/shard_map/ppermute | solution.py:40
  19.6 0.0 collective-permute-done.2.refs_3_
  19.6 0.0 collective-permute-done.4.refs_5_
  19.6 0.0 collective-permute-done.5.refs_6_
  19.6 0.0 collective-permute-done.6.refs_7_
  19.6 1.6 %adam.1 = (f32[1,256,128]{2,1,0:T(8,128)}, f32[1,256,128]{2,1,0:T(8,128)}, f32[1,256,128]{2,1,0:T(8,128)}) custom-call(s32[4,4]{1,0:T(4,128)S(1)} %copy-done.5, s32[4,4]{1,0:T(4,128)S(1)} %copy-done.6, s32[4]{0:T(128)S(1)} %copy-done.7, f32[3,64,128]{2,1,0:T(8,128)S(1)} %get-tuple-element.11.refs_0_, f32[3,64,128]{2,1,0:T(8,128)S(1)} %collective-permute-done.refs_1_, ...), custom_call_target="tpu_custom_call" | custom-call | tf_op jit(solution)/shard_map/adam/pallas_call | solution.py:212
  (10 shorter events, 0.1 us)
Async XLA Ops:
  0.6 1.0 %copy-start = (bf16[1,2048,128]{2,1,0:T(8,128)(2,1)S(1)}, bf16[1,2048,128]{2,1,0:T(8,128)(2,1)}, u32[]{:S(2)}) copy-start(bf16[1,2048,128]{2,1,0:T(8,128)(2,1)} %param.10) | copy-start | bytes 1572868
  1.7 0.8 %copy-start.2 = (f32[1,128,128]{2,1,0:T(8,128)S(1)}, f32[1,128,128]{2,1,0:T(8,128)}, u32[]{:S(2)}) copy-start(f32[1,128,128]{2,1,0:T(8,128)} %w.1) | copy-start | bytes 196612
  1.7 0.9 %copy-start.3 = (f32[1,128,128]{2,1,0:T(8,128)S(1)}, f32[1,128,128]{2,1,0:T(8,128)}, u32[]{:S(2)}) copy-start(f32[1,128,128]{2,1,0:T(8,128)} %m.1) | copy-start | bytes 196612
  1.7 0.9 %copy-start.4 = (f32[1,128,128]{2,1,0:T(8,128)S(1)}, f32[1,128,128]{2,1,0:T(8,128)}, u32[]{:S(2)}) copy-start(f32[1,128,128]{2,1,0:T(8,128)} %v.1) | copy-start | bytes 196612
  1.7 0.9 %copy-start.5 = (s32[4,4]{1,0:T(4,128)S(1)}, s32[4,4]{1,0:T(4,128)}, u32[]{:S(2)}) copy-start(s32[4,4]{1,0:T(4,128)} %owner.3) | copy-start | bytes 196
  1.7 0.9 %copy-start.6 = (s32[4,4]{1,0:T(4,128)S(1)}, s32[4,4]{1,0:T(4,128)}, u32[]{:S(2)}) copy-start(s32[4,4]{1,0:T(4,128)} %lengths.3) | copy-start | bytes 196
  1.7 0.9 %copy-start.7 = (s32[4]{0:T(128)S(1)}, s32[4]{0:T(128)}, u32[]{:S(2)}) copy-start(s32[4]{0:T(128)} %worker.3) | copy-start | bytes 52
  1.7 4.7 %copy-start.1 = (bf16[1,2048,128]{2,1,0:T(8,128)(2,1)S(1)}, bf16[1,2048,128]{2,1,0:T(8,128)(2,1)}, u32[]{:S(2)}) copy-start(bf16[1,2048,128]{2,1,0:T(8,128)(2,1)} %param.10) | copy-start | bytes 1572868
  1.8 4.6 %collective-permute-start.3 = (f32[4,256,128]{2,1,0:T(8,128)S(1)}, f32[4,256,128]{2,1,0:T(8,128)S(1)}, u32[]{:S(2)}, u32[]{:S(2)}) collective-permute-start(f32[4,256,128]{2,1,0:T(8,128)S(1)} %widen.1), channel_id=1, source_target_pairs={{0,1},{1,0},{2,3},{3,2},{4,5},{5,4},{6,7},{7,6},{8,9},{9,8},{10,11... | collective-permute-start | bytes 1572872 | tf_op jit(solution)/shard_map/ppermute | solution.py:40
  3.2 9.3 %collective-permute-start = (f32[3,64,128]{2,1,0:T(8,128)S(1)}, f32[3,64,128]{2,1,0:T(8,128)S(1)}, u32[]{:S(2)}, u32[]{:S(2)}) collective-permute-start(f32[3,64,128]{2,1,0:T(8,128)S(1)} %get-tuple-element.12), channel_id=1, source_target_pairs={{0,2},{2,0},{4,6},{6,4},{1,3},{3,1},{5,7},{7,5},{8,10},{10,8},{12,... | collective-permute-start | bytes 294920 | tf_op jit(solution)/shard_map/ppermute | solution.py:40
  6.4 13.1 %collective-permute-start.4 = (f32[256,128]{1,0:T(8,128)S(1)}, f32[256,128]{1,0:T(8,128)S(1)}, u32[]{:S(2)}, u32[]{:S(2)}) collective-permute-start(f32[256,128]{1,0:T(8,128)S(1)} %get-tuple-element.16), channel_id=1, source_target_pairs={{0,8},{8,0},{16,24},{24,16},{1,9},{9,1},{17,25},{25,17},{2,10},{10... | collective-permute-start | bytes 393224 | tf_op jit(solution)/shard_map/ppermute | solution.py:40
  8.0 11.6 %collective-permute-start.5 = (f32[256,128]{1,0:T(8,128)S(1)}, f32[256,128]{1,0:T(8,128)S(1)}, u32[]{:S(2)}, u32[]{:S(2)}) collective-permute-start(f32[256,128]{1,0:T(8,128)S(1)} %get-tuple-element.17), channel_id=1, source_target_pairs={{0,16},{8,24},{16,0},{24,8},{1,17},{9,25},{17,1},{25,9},{2,18},{10... | collective-permute-start | bytes 393224 | tf_op jit(solution)/shard_map/ppermute | solution.py:40
  9.5 10.1 %collective-permute-start.6 = (f32[256,128]{1,0:T(8,128)S(1)}, f32[256,128]{1,0:T(8,128)S(1)}, u32[]{:S(2)}, u32[]{:S(2)}) collective-permute-start(f32[256,128]{1,0:T(8,128)S(1)} %get-tuple-element.18), channel_id=1, source_target_pairs={{0,24},{8,16},{16,8},{24,0},{1,25},{9,17},{17,9},{25,1},{2,26},{10... | collective-permute-start | bytes 393224 | tf_op jit(solution)/shard_map/ppermute | solution.py:40
  10.0 9.6 %collective-permute-start.1 = (f32[3,64,128]{2,1,0:T(8,128)S(1)}, f32[3,64,128]{2,1,0:T(8,128)S(1)}, u32[]{:S(2)}, u32[]{:S(2)}) collective-permute-start(f32[3,64,128]{2,1,0:T(8,128)S(1)} %get-tuple-element.13), channel_id=1, source_target_pairs={{0,4},{2,6},{4,0},{6,2},{1,5},{3,7},{5,1},{7,3},{8,12},{10,14},{12... | collective-permute-start | bytes 294920 | tf_op jit(solution)/shard_map/ppermute | solution.py:40
  12.6 7.0 %collective-permute-start.2 = (f32[3,64,128]{2,1,0:T(8,128)S(1)}, f32[3,64,128]{2,1,0:T(8,128)S(1)}, u32[]{:S(2)}, u32[]{:S(2)}) collective-permute-start(f32[3,64,128]{2,1,0:T(8,128)S(1)} %get-tuple-element.14), channel_id=1, source_target_pairs={{0,6},{2,4},{4,2},{6,0},{1,7},{3,5},{5,3},{7,1},{8,14},{10,12},{12... | collective-permute-start | bytes 294920 | tf_op jit(solution)/shard_map/ppermute | solution.py:40
